TPU v7x, 256 devices: a whole 4x4x8 slice. The times are simulated.
256 devices in a mesh: gz: 4 (over x), grid: 64 (over y, z, core).
Axes of the slice: x: 4, y: 4, z: 8, core: 2. Of those that a mesh axis runs over, the one named last changes fastest.
Arguments:
- rhs: bfloat16 [6, 128, 32, 128], P(None, 'grid'), may hold values from -6 to 6
- lower_updates: bfloat16 [4, 6, 128, 32, 128], P('gz', None, 'grid'), may hold values from -6 to 6
- diag_inv: bfloat16 [6, 128, 128, 128], P(None, 'grid'), may hold values from -0.5 to 0.5
- lower_blocks: bfloat16 [5, 128, 128, 128], P(None, 'grid'), may hold values from -0.5 to 0.5
- upper_inv: bfloat16 [6, 128, 128, 128], P(None, 'grid'), may hold values from -0.5 to 0.5
- upper_blocks: bfloat16 [5, 128, 128, 128], P(None, 'grid'), may hold values from -0.5 to 0.5
- parent: int32 [5, 128], P(None, 'grid'), may hold values from 0 to 127, as said below
- live_count: int32 [6, 64], P(None, 'grid'), may hold values from 1 to 2
Outputs:
- solution: bfloat16 [6, 128, 32, 128], P(None, 'grid')
Inputs may be any that keep to these rules, and one draw needn't show every extreme that they name: At level l the slots form aligned groups of S = min(128, 4 * 2 * 2 ** l) slots (those of min(64, 4 * 2 ** l) grid indices in a row); parent[l, g] lies in the group of g, between (g // S) * S and (g // S) * S + S - 1, and both ends are named in every group.
All inputs are finite; a program needn't handle non-finite values.
Results may differ from a plain program's by a relative error of at most 0.03.
Values may be sent and summed in bfloat16 or wider, within the bound.
A program may use at most 64 MiB of HBM per device.

v0:
```python
import jax
import jax.numpy as jnp
from jax import lax
from jax.sharding import PartitionSpec as P


def on_device(
    rhs, lower_updates, diag_inv, lower_blocks, upper_inv, upper_blocks, parent, live_count
):
    f32 = jnp.float32
    bf16 = jnp.bfloat16
    levels, slots, rows, width = rhs.shape
    own_slots = lax.axis_index("grid") * slots + jnp.arange(slots, dtype=jnp.int32)
    live = (jnp.arange(slots, dtype=jnp.int32)[None, :] < live_count).astype(f32)
    updates = lax.psum(lower_updates[0].astype(f32).astype(jnp.bfloat16), "gz").astype(jnp.float32)
    flat = rows * width
    incoming = jnp.zeros((slots, rows, width), f32)
    forward_all = []
    for level in range(levels):
        residual = (rhs[level].astype(f32) - updates[level] - incoming).astype(bf16)
        forward = jnp.einsum("srw,swv->srv", residual, diag_inv[level], preferred_element_type=f32)
        forward = (forward * live[level][:, None, None]).astype(bf16)
        forward_all.append(forward)
        if level + 1 < levels:
            sent = jnp.einsum(
                "srw,swv->srv", forward, lower_blocks[level], preferred_element_type=f32
            )
            sent = sent.astype(bf16).reshape(slots, flat)
            targets = parent[level]
            values = lax.all_gather(sent, "grid", axis=0, tiled=True)
            owners = lax.all_gather(targets, "grid", axis=0, tiled=True)
            onehot = (owners[None, :] == own_slots[:, None]).astype(bf16)
            summed = jnp.dot(onehot, values, preferred_element_type=f32)
            incoming = summed.reshape(slots, rows, width)
    answer = [None] * levels
    upper_flat = None
    for level in range(levels - 1, -1, -1):
        if level == levels - 1:
            target = forward_all[level].astype(f32)
        else:
            targets = parent[level]

            def select_parent(total, piece, first, targets=targets):
                wanted = jnp.arange(piece.shape[0], dtype=jnp.int32)
                chosen = (targets[:, None] == wanted[None, :]).astype(bf16)
                return jnp.dot(chosen, piece, preferred_element_type=f32)

            above = select_parent(
                jnp.zeros((slots, flat), f32),
                lax.all_gather(upper_flat, "grid", axis=0, tiled=True),
                jnp.int32(0),
            )
            above = above.astype(bf16).reshape(slots, rows, width)
            target = forward_all[level].astype(f32) - jnp.einsum(
                "srw,swv->srv", above, upper_blocks[level], preferred_element_type=f32
            )
        target = target.astype(bf16)
        result = jnp.einsum("srw,swv->srv", target, upper_inv[level], preferred_element_type=f32)
        solved = (result * live[level][:, None, None]).astype(bf16)
        answer[level] = solved
        upper_flat = solved.reshape(slots, flat)
    stacked = jnp.stack(answer)
    return stacked


def solution(mesh):
    return jax.shard_map(
        on_device,
        mesh=mesh,
        in_specs=(
            P(None, "grid", None, None),
            P("gz", None, "grid", None, None),
            P(None, "grid", None, None),
            P(None, "grid", None, None),
            P(None, "grid", None, None),
            P(None, "grid", None, None),
            P(None, "grid"),
            P(None, "grid"),
        ),
        out_specs=P(None, "grid", None, None),
        check_vma=False,
    )
```

profile of v0, /device:TPU:1, one launch (start us, length us, event | category | flops | bytes accessed | tf_op | source)
XLA Modules:
  0.0 849.4 jit_solution(444018859633957401)
XLA Ops:
  6.5 0.7 all-reduce.8.cloned.1.call-update
  7.3 0.7 fusion.132
  8.0 49.8 %all-reduce.8.cloned.1.call-done = bf16[6,2,32,128]{3,2,1,0:T(8,128)(2,1)} async-done(((bf16[6,2,32,128]{3,2,1,0:T(8,128)(2,1)}), bf16[6,2,32,128]{3,2,1,0:T(8,128)(2,1)}) %all-reduce.8.cloned.1.call-update) | async-done | bytes 98320 | tf_op jit(solution)/shard_map/psum | solution.py:15
  57.8 0.9 convert_element_type.162
  58.7 0.8 fusion
  59.5 1.0 convolution_convert_fusion.9
  60.5 0.6 reshape.133
  61.3 0.7 copy-done.7
  61.9 0.6 dynamic-slice
  63.2 0.2 slice_reduce_fusion
  63.5 0.2 dynamic-update-slice.4
  63.7 0.2 dynamic-update-slice.2
  63.9 0.2 dynamic-update-slice.1
  64.5 19.4 %all-reduce.5 = (s32[128]{0:T(128)S(1)}, s32[128]{0:T(128)S(1)}, s32[128]{0:T(128)S(1)}, s32[128]{0:T(128)S(1)}, s32[128]{0:T(128)S(1)}) all-reduce(s32[128]{0:T(128)S(1)} %dynamic-update-slice, s32[128]{0:T(128)S(1)} %dynamic-update-slice.1, s32[128]{0:T(128)S(1)} %dynamic-update-slice.2, ...), channel_id=2, replica_groups=mesh['gz'=4,'grid'=64] {'grid'}, use_global_device_ids=true, to_apply=%add | all-reduce | flops 640 | bytes 5120
  83.9 57.2 %all-gather.26.cloned.1.call-done = bf16[64,2,4096]{2,1,0:T(2,128)(2,1)} async-done(((bf16[1,2,4096]{2,1,0:T(2,128)(2,1)}), bf16[64,2,4096]{2,1,0:T(2,128)(2,1)}) %all-gather.26.cloned.1.call-update) | async-done | bytes 1048592 | tf_op jit(solution)/shard_map/all_gather | solution.py:30
  141.1 1.5 reshape.134
  142.6 0.3 convolution_bitcast_fusion.4
  142.9 0.6 copy-done.2
  143.7 0.6 reshape.135
  144.4 74.7 %all-gather.28.cloned.1.call-done = bf16[64,2,4096]{2,1,0:T(2,128)(2,1)} async-done(((bf16[1,2,4096]{2,1,0:T(2,128)(2,1)}), bf16[64,2,4096]{2,1,0:T(2,128)(2,1)}) %all-gather.28.cloned.1.call-update) | async-done | bytes 1048592 | tf_op jit(solution)/shard_map/all_gather | solution.py:30
  219.1 1.5 reshape.136
  220.5 0.3 convolution_bitcast_fusion.3
  221.1 0.6 reshape.137
  221.8 74.7 %all-gather.30.cloned.1.call-done = bf16[64,2,4096]{2,1,0:T(2,128)(2,1)} async-done(((bf16[1,2,4096]{2,1,0:T(2,128)(2,1)}), bf16[64,2,4096]{2,1,0:T(2,128)(2,1)}) %all-gather.30.cloned.1.call-update) | async-done | bytes 1048592 | tf_op jit(solution)/shard_map/all_gather | solution.py:30
  296.5 1.5 reshape.138
  297.9 0.3 convolution_bitcast_fusion.2
  298.5 0.6 reshape.139
  299.2 74.7 %all-gather.32.cloned.1.call-done = bf16[64,2,4096]{2,1,0:T(2,128)(2,1)} async-done(((bf16[1,2,4096]{2,1,0:T(2,128)(2,1)}), bf16[64,2,4096]{2,1,0:T(2,128)(2,1)}) %all-gather.32.cloned.1.call-update) | async-done | bytes 1048592 | tf_op jit(solution)/shard_map/all_gather | solution.py:30
  373.9 1.5 reshape.140
  375.4 0.3 convolution_bitcast_fusion.1
  375.9 0.6 reshape.141
  376.6 74.7 %all-gather.34.cloned.1.call-done = bf16[64,2,4096]{2,1,0:T(2,128)(2,1)} async-done(((bf16[1,2,4096]{2,1,0:T(2,128)(2,1)}), bf16[64,2,4096]{2,1,0:T(2,128)(2,1)}) %all-gather.34.cloned.1.call-update) | async-done | bytes 1048592 | tf_op jit(solution)/shard_map/all_gather | solution.py:30
  451.3 1.5 reshape.142
  452.8 0.3 convolution_bitcast_fusion
  453.1 0.7 copy-done.4
  453.8 0.2 fusion.6
  454.0 0.7 reshape.143
  454.7 74.7 %all-gather.36.cloned.1.call-done = bf16[64,2,4096]{2,1,0:T(2,128)(2,1)} async-done(((bf16[1,2,4096]{2,1,0:T(2,128)(2,1)}), bf16[64,2,4096]{2,1,0:T(2,128)(2,1)}) %all-gather.36.cloned.1.call-update) | async-done | bytes 1048592 | tf_op jit(solution)/shard_map/all_gather | solution.py:50
  529.4 1.5 reshape.144
  530.8 0.3 fusion.19
  531.1 0.7 copy-done.5
  531.8 0.2 fusion.8
  532.0 0.7 reshape.145
  532.8 74.7 %all-gather.38.cloned.1.call-done = bf16[64,2,4096]{2,1,0:T(2,128)(2,1)} async-done(((bf16[1,2,4096]{2,1,0:T(2,128)(2,1)}), bf16[64,2,4096]{2,1,0:T(2,128)(2,1)}) %all-gather.38.cloned.1.call-update) | async-done | bytes 1048592 | tf_op jit(solution)/shard_map/all_gather | solution.py:50
  607.4 1.5 reshape.146
  608.9 0.3 fusion.20
  609.2 0.2 fusion.10
  609.4 0.7 reshape.147
  610.1 74.7 %all-gather.40.cloned.1.call-done = bf16[64,2,4096]{2,1,0:T(2,128)(2,1)} async-done(((bf16[1,2,4096]{2,1,0:T(2,128)(2,1)}), bf16[64,2,4096]{2,1,0:T(2,128)(2,1)}) %all-gather.40.cloned.1.call-update) | async-done | bytes 1048592 | tf_op jit(solution)/shard_map/all_gather | solution.py:50
  684.8 1.5 reshape.148
  686.3 0.3 fusion.21
  686.6 0.2 fusion.12
  686.8 0.7 reshape.149
  687.5 74.7 %all-gather.42.cloned.1.call-done = bf16[64,2,4096]{2,1,0:T(2,128)(2,1)} async-done(((bf16[1,2,4096]{2,1,0:T(2,128)(2,1)}), bf16[64,2,4096]{2,1,0:T(2,128)(2,1)}) %all-gather.42.cloned.1.call-update) | async-done | bytes 1048592 | tf_op jit(solution)/shard_map/all_gather | solution.py:50
  762.2 1.5 reshape.150
  763.7 0.3 fusion.22
  764.0 0.2 fusion.14
  764.2 0.7 reshape.151
  764.9 74.7 %all-gather.44.cloned.1.call-done = bf16[64,2,4096]{2,1,0:T(2,128)(2,1)} async-done(((bf16[1,2,4096]{2,1,0:T(2,128)(2,1)}), bf16[64,2,4096]{2,1,0:T(2,128)(2,1)}) %all-gather.44.cloned.1.call-update) | async-done | bytes 1048592 | tf_op jit(solution)/shard_map/all_gather | solution.py:50
  839.6 1.5 reshape.152
  841.0 0.3 fusion.23
  841.4 0.2 fusion.18
  841.7 0.6 copy-done.6
  842.3 0.6 bitcast_dynamic-update-slice_fusion
  (53 shorter events, 2.2 us)
Async XLA Ops:
  6.5 52.2 %copy-start = (bf16[6,2,128,128]{3,2,1,0:T(8,128)(2,1)S(1)}, bf16[6,2,128,128]{3,2,1,0:T(8,128)(2,1)}, u32[]{:S(2)}) copy-start(bf16[6,2,128,128]{3,2,1,0:T(8,128)(2,1)} %param.10) | copy-start | bytes 1179652
  6.5 51.3 %all-reduce.8.cloned.1.call-start = ((), (), s32[]{:S(2)}) async-start(), calls=%async_computation | async-start | bytes 196608 | tf_op jit(solution)/shard_map/psum | solution.py:15
  7.3 133.8 %all-gather.26.cloned.1.call-start = ((), (), s32[]{:S(2)}) async-start(), calls=%async_computation.1 | async-start | bytes 1064960 | tf_op jit(solution)/shard_map/all_gather | solution.py:30
  61.2 157.9 %all-gather.28.cloned.1.call-start = ((), (), s32[]{:S(2)}) async-start(), calls=%async_computation.2 | async-start | bytes 1064960 | tf_op jit(solution)/shard_map/all_gather | solution.py:30
  61.2 0.7 copy-start.7
  62.5 0.7 copy-start.3
  142.5 0.9 copy-start.2
  142.6 1.0 copy-start.1
  144.4 152.1 %all-gather.30.cloned.1.call-start = ((), (), s32[]{:S(2)}) async-start(), calls=%async_computation.3 | async-start | bytes 1064960 | tf_op jit(solution)/shard_map/all_gather | solution.py:30
  221.8 152.1 %all-gather.32.cloned.1.call-start = ((), (), s32[]{:S(2)}) async-start(), calls=%async_computation.4 | async-start | bytes 1064960 | tf_op jit(solution)/shard_map/all_gather | solution.py:30
  299.2 152.1 %all-gather.34.cloned.1.call-start = ((), (), s32[]{:S(2)}) async-start(), calls=%async_computation.5 | async-start | bytes 1064960 | tf_op jit(solution)/shard_map/all_gather | solution.py:30
  376.6 152.8 %all-gather.36.cloned.1.call-start = ((), (), s32[]{:S(2)}) async-start(), calls=%async_computation.6 | async-start | bytes 1064960 | tf_op jit(solution)/shard_map/all_gather | solution.py:50
  452.8 1.0 copy-start.4
  454.7 152.8 %all-gather.38.cloned.1.call-start = ((), (), s32[]{:S(2)}) async-start(), calls=%async_computation.7 | async-start | bytes 1064960 | tf_op jit(solution)/shard_map/all_gather | solution.py:50
  530.8 1.0 copy-start.5
  532.7 152.1 %all-gather.40.cloned.1.call-start = ((), (), s32[]{:S(2)}) async-start(), calls=%async_computation.8 | async-start | bytes 1064960 | tf_op jit(solution)/shard_map/all_gather | solution.py:50
  610.1 152.1 %all-gather.42.cloned.1.call-start = ((), (), s32[]{:S(2)}) async-start(), calls=%async_computation.9 | async-start | bytes 1064960 | tf_op jit(solution)/shard_map/all_gather | solution.py:50
  687.5 152.1 %all-gather.44.cloned.1.call-start = ((), (), s32[]{:S(2)}) async-start(), calls=%async_computation.10 | async-start | bytes 1064960 | tf_op jit(solution)/shard_map/all_gather | solution.py:50
  841.7 0.6 copy-start.6
Sparse Core Ops, SparseCore 0:
  9.6 48.1 all-reduce.7
  61.3 79.7 all-gather.25
  144.5 74.5 all-gather.27
  221.9 74.5 all-gather.29
  299.3 74.5 all-gather.31
  376.7 74.5 all-gather.33
  454.8 74.5 all-gather.35
  532.8 74.5 all-gather.37
  610.2 74.5 all-gather.39
  687.6 74.5 all-gather.41
  765.0 74.5 all-gather.43
where the time goes:
time: 850 us; the launch traced here: 849 us
  waiting for transfers between devices  780 us (92%)
  local copies, waits for them, and re-layouts  27 us (3%)
  blocking collectives  19.4 us (2%)
  between operations  14.1 us (2%)
    all_gather x5, waiting for transfers between devices, on_device(): lax.all_gather(upper_flat, 'grid', axis=0, tiled=True)  373 us
    all_gather x5, waiting for transfers between devices, on_device(): values = lax.all_gather(sent, 'grid', axis=0, tiled=True)  356 us
    psum x1, waiting for transfers between devices, on_device(): lax.psum(lower_updates[0].astype(f32).astype(jnp.bfloat16), 'gz')  49.8 us
    unnamed x51, local copies, waits for them, and re-layouts  26.1 us
    unnamed x1, blocking collectives  19.4 us
  transfers between devices with their start and end apart: 11, of which 11 were waited for; matrix products, arithmetic and copies ran while one was open for 0% of the time, Pallas kernels for 0%

commit v1 on v0

--- a/solution.py
+++ b/solution.py
@@ -12,7 +12,9 @@
     levels, slots, rows, width = rhs.shape
     own_slots = lax.axis_index("grid") * slots + jnp.arange(slots, dtype=jnp.int32)
     live = (jnp.arange(slots, dtype=jnp.int32)[None, :] < live_count).astype(f32)
-    updates = lax.psum(lower_updates[0].astype(f32).astype(jnp.bfloat16), "gz").astype(jnp.float32)
+    updates = jnp.sum(
+        lax.all_gather(lower_updates[0].astype(f32).astype(jnp.bfloat16), "gz"), axis=0
+    ).astype(jnp.float32)
     flat = rows * width
     incoming = jnp.zeros((slots, rows, width), f32)
     forward_all = []

time: 850 us -> 812 us (0.955)
  waiting for transfers between devices: 780 us -> 729 us
  blocking collectives: 19.4 us -> 34 us
    psum x1 -> x0, waiting for transfers between devices: 49.8 us -> none  [on_device(): lax.psum(lower_updates[0].astype(f32).astype(jnp.bfloat16), 'gz')]
    all_gather x0 -> x1, blocking collectives: none -> 11.9 us  [on_device(): lax.all_gather(lower_updates[0].astype(f32).astype(jnp.bfloat16), 'gz')]
    unnamed x51 -> x53, local copies, waits for them, and re-layouts: 26.1 us -> 27.2 us
  transfers between devices with their start and end apart: 11 -> 10, of which waited for: 11 -> 10; matrix products, arithmetic and copies ran while one was open for 0% -> 0% of each run, Pallas kernels for 0% -> 0%
where the time goes in v1:
time: 812 us; the launch traced here: 811 us
  waiting for transfers between devices  729 us (90%)
  blocking collectives  34 us (4%)
  local copies, waits for them, and re-layouts  28 us (3%)
  between operations  14.3 us (2%)
    all_gather x5, waiting for transfers between devices, on_device(): lax.all_gather(upper_flat, 'grid', axis=0, tiled=True)  373 us
    all_gather x5, waiting for transfers between devices, on_device(): values = lax.all_gather(sent, 'grid', axis=0, tiled=True)  355 us
    unnamed x53, local copies, waits for them, and re-layouts  27.2 us
    unnamed x1, blocking collectives  22.1 us
  transfers between devices with their start and end apart: 10, of which 10 were waited for; matrix products, arithmetic and copies ran while one was open for 0% of the time, Pallas kernels for 0%

profile of v1, /device:TPU:1, one launch (start us, length us, event | category | flops | bytes accessed | tf_op | source)
XLA Modules:
  0.0 811.3 jit_solution(809467203784156283)
XLA Ops:
  6.5 0.7 copy-done.5
  7.3 11.9 %all_gather.49 = bf16[4,6,2,32,128]{4,3,2,1,0:T(8,128)(2,1)S(1)} all-gather(bf16[1,6,2,32,128]{4,3,2,1,0:T(8,128)(2,1)} %param.9), channel_id=1, replica_groups=mesh['gz'=4,'grid'=64] {'gz'}, dimensions={0}, use_global_device_ids=true | all-gather | bytes 491520 | tf_op jit(solution)/shard_map/all_gather | solution.py:16
  19.3 0.9 copy-done
  20.5 0.6 reshape.134
  21.2 0.7 copy-done.8
  21.8 0.6 dynamic-slice
  23.1 0.2 slice_reduce_fusion
  23.3 0.2 dynamic-update-slice.4
  23.6 0.2 dynamic-update-slice.2
  23.8 0.2 dynamic-update-slice.1
  24.0 0.2 dynamic-update-slice
  24.2 0.2 dynamic-update-slice.3
  24.4 22.1 %all-reduce.5 = (s32[128]{0:T(128)S(1)}, s32[128]{0:T(128)S(1)}, s32[128]{0:T(128)S(1)}, s32[128]{0:T(128)S(1)}, s32[128]{0:T(128)S(1)}) all-reduce(s32[128]{0:T(128)S(1)} %dynamic-update-slice, s32[128]{0:T(128)S(1)} %dynamic-update-slice.1, s32[128]{0:T(128)S(1)} %dynamic-update-slice.2, ...), channel_id=2, replica_groups=mesh['gz'=4,'grid'=64] {'grid'}, use_global_device_ids=true, to_apply=%add | all-reduce | flops 640 | bytes 5120
  46.5 56.7 %all-gather.26.cloned.1.call-done = bf16[64,2,4096]{2,1,0:T(2,128)(2,1)} async-done(((bf16[1,2,4096]{2,1,0:T(2,128)(2,1)}), bf16[64,2,4096]{2,1,0:T(2,128)(2,1)}) %all-gather.26.cloned.1.call-update) | async-done | bytes 1048592 | tf_op jit(solution)/shard_map/all_gather | solution.py:32
  103.2 1.5 reshape.135
  104.7 0.3 convolution_bitcast_fusion.4
  105.1 0.2 convolution_convert_fusion.8
  105.3 0.6 reshape.136
  106.0 74.7 %all-gather.28.cloned.1.call-done = bf16[64,2,4096]{2,1,0:T(2,128)(2,1)} async-done(((bf16[1,2,4096]{2,1,0:T(2,128)(2,1)}), bf16[64,2,4096]{2,1,0:T(2,128)(2,1)}) %all-gather.28.cloned.1.call-update) | async-done | bytes 1048592 | tf_op jit(solution)/shard_map/all_gather | solution.py:32
  180.6 1.5 reshape.137
  182.1 0.3 convolution_bitcast_fusion.3
  182.5 0.2 convolution_convert_fusion.7
  182.7 0.6 reshape.138
  183.4 74.7 %all-gather.30.cloned.1.call-done = bf16[64,2,4096]{2,1,0:T(2,128)(2,1)} async-done(((bf16[1,2,4096]{2,1,0:T(2,128)(2,1)}), bf16[64,2,4096]{2,1,0:T(2,128)(2,1)}) %all-gather.30.cloned.1.call-update) | async-done | bytes 1048592 | tf_op jit(solution)/shard_map/all_gather | solution.py:32
  258.0 1.5 reshape.139
  259.5 0.3 convolution_bitcast_fusion.2
  260.1 0.6 reshape.140
  260.8 74.7 %all-gather.32.cloned.1.call-done = bf16[64,2,4096]{2,1,0:T(2,128)(2,1)} async-done(((bf16[1,2,4096]{2,1,0:T(2,128)(2,1)}), bf16[64,2,4096]{2,1,0:T(2,128)(2,1)}) %all-gather.32.cloned.1.call-update) | async-done | bytes 1048592 | tf_op jit(solution)/shard_map/all_gather | solution.py:32
  335.4 1.5 reshape.141
  336.9 0.3 convolution_bitcast_fusion.1
  337.5 0.6 reshape.142
  338.2 74.7 %all-gather.34.cloned.1.call-done = bf16[64,2,4096]{2,1,0:T(2,128)(2,1)} async-done(((bf16[1,2,4096]{2,1,0:T(2,128)(2,1)}), bf16[64,2,4096]{2,1,0:T(2,128)(2,1)}) %all-gather.34.cloned.1.call-update) | async-done | bytes 1048592 | tf_op jit(solution)/shard_map/all_gather | solution.py:32
  412.8 1.5 reshape.143
  414.3 0.3 convolution_bitcast_fusion
  414.6 0.7 copy-done.4
  415.3 0.2 fusion.6
  415.5 0.7 reshape.144
  416.3 74.7 %all-gather.36.cloned.1.call-done = bf16[64,2,4096]{2,1,0:T(2,128)(2,1)} async-done(((bf16[1,2,4096]{2,1,0:T(2,128)(2,1)}), bf16[64,2,4096]{2,1,0:T(2,128)(2,1)}) %all-gather.36.cloned.1.call-update) | async-done | bytes 1048592 | tf_op jit(solution)/shard_map/all_gather | solution.py:52
  490.9 1.5 reshape.145
  492.4 0.3 fusion.19
  492.7 0.7 copy-done.6
  493.4 0.2 fusion.8
  493.6 0.7 reshape.146
  494.3 74.7 %all-gather.38.cloned.1.call-done = bf16[64,2,4096]{2,1,0:T(2,128)(2,1)} async-done(((bf16[1,2,4096]{2,1,0:T(2,128)(2,1)}), bf16[64,2,4096]{2,1,0:T(2,128)(2,1)}) %all-gather.38.cloned.1.call-update) | async-done | bytes 1048592 | tf_op jit(solution)/shard_map/all_gather | solution.py:52
  569.0 1.5 reshape.147
  570.4 0.3 fusion.20
  570.7 0.2 fusion.10
  571.0 0.7 reshape.148
  571.7 74.7 %all-gather.40.cloned.1.call-done = bf16[64,2,4096]{2,1,0:T(2,128)(2,1)} async-done(((bf16[1,2,4096]{2,1,0:T(2,128)(2,1)}), bf16[64,2,4096]{2,1,0:T(2,128)(2,1)}) %all-gather.40.cloned.1.call-update) | async-done | bytes 1048592 | tf_op jit(solution)/shard_map/all_gather | solution.py:52
  646.4 1.5 reshape.149
  647.8 0.3 fusion.21
  648.1 0.2 fusion.12
  648.3 0.7 reshape.150
  649.1 74.7 %all-gather.42.cloned.1.call-done = bf16[64,2,4096]{2,1,0:T(2,128)(2,1)} async-done(((bf16[1,2,4096]{2,1,0:T(2,128)(2,1)}), bf16[64,2,4096]{2,1,0:T(2,128)(2,1)}) %all-gather.42.cloned.1.call-update) | async-done | bytes 1048592 | tf_op jit(solution)/shard_map/all_gather | solution.py:52
  723.7 1.5 reshape.151
  725.2 0.3 fusion.22
  725.5 0.2 fusion.14
  725.7 0.7 reshape.152
  726.4 74.7 %all-gather.44.cloned.1.call-done = bf16[64,2,4096]{2,1,0:T(2,128)(2,1)} async-done(((bf16[1,2,4096]{2,1,0:T(2,128)(2,1)}), bf16[64,2,4096]{2,1,0:T(2,128)(2,1)}) %all-gather.44.cloned.1.call-update) | async-done | bytes 1048592 | tf_op jit(solution)/shard_map/all_gather | solution.py:52
  801.1 1.5 reshape.153
  802.6 0.3 fusion.23
  802.9 0.2 fusion.18
  803.2 0.6 copy-done.7
  803.8 0.6 bitcast_dynamic-update-slice_fusion
  (54 shorter events, 1.9 us)
Async XLA Ops:
  6.5 0.7 copy-start.5
  6.5 96.7 %all-gather.26.cloned.1.call-start = ((), (), s32[]{:S(2)}) async-start(), calls=%async_computation | async-start | bytes 1064960 | tf_op jit(solution)/shard_map/all_gather | solution.py:32
  19.2 1.0 copy-start
  19.2 1.0 copy-start.2
  19.2 1.1 copy-start.1
  21.1 159.5 %all-gather.28.cloned.1.call-start = ((), (), s32[]{:S(2)}) async-start(), calls=%async_computation.1 | async-start | bytes 1064960 | tf_op jit(solution)/shard_map/all_gather | solution.py:32
  21.2 0.7 copy-start.8
  22.4 0.7 copy-start.3
  105.9 152.1 %all-gather.30.cloned.1.call-start = ((), (), s32[]{:S(2)}) async-start(), calls=%async_computation.2 | async-start | bytes 1064960 | tf_op jit(solution)/shard_map/all_gather | solution.py:32
  183.3 152.1 %all-gather.32.cloned.1.call-start = ((), (), s32[]{:S(2)}) async-start(), calls=%async_computation.3 | async-start | bytes 1064960 | tf_op jit(solution)/shard_map/all_gather | solution.py:32
  260.7 152.1 %all-gather.34.cloned.1.call-start = ((), (), s32[]{:S(2)}) async-start(), calls=%async_computation.4 | async-start | bytes 1064960 | tf_op jit(solution)/shard_map/all_gather | solution.py:32
  338.1 152.8 %all-gather.36.cloned.1.call-start = ((), (), s32[]{:S(2)}) async-start(), calls=%async_computation.5 | async-start | bytes 1064960 | tf_op jit(solution)/shard_map/all_gather | solution.py:52
  414.3 1.0 copy-start.4
  416.2 152.8 %all-gather.38.cloned.1.call-start = ((), (), s32[]{:S(2)}) async-start(), calls=%async_computation.6 | async-start | bytes 1064960 | tf_op jit(solution)/shard_map/all_gather | solution.py:52
  492.4 1.0 copy-start.6
  494.3 152.1 %all-gather.40.cloned.1.call-start = ((), (), s32[]{:S(2)}) async-start(), calls=%async_computation.7 | async-start | bytes 1064960 | tf_op jit(solution)/shard_map/all_gather | solution.py:52
  571.6 152.1 %all-gather.42.cloned.1.call-start = ((), (), s32[]{:S(2)}) async-start(), calls=%async_computation.8 | async-start | bytes 1064960 | tf_op jit(solution)/shard_map/all_gather | solution.py:52
  649.0 152.1 %all-gather.44.cloned.1.call-start = ((), (), s32[]{:S(2)}) async-start(), calls=%async_computation.9 | async-start | bytes 1064960 | tf_op jit(solution)/shard_map/all_gather | solution.py:52
  803.2 0.6 copy-start.7
Sparse Core Ops, SparseCore 0:
  21.2 81.9 all-gather.25
  106.0 74.5 all-gather.27
  183.4 74.5 all-gather.29
  260.8 74.5 all-gather.31
  338.2 74.5 all-gather.33
  416.3 74.5 all-gather.35
  494.4 74.5 all-gather.37
  571.8 74.5 all-gather.39
  649.2 74.5 all-gather.41
  726.5 74.5 all-gather.43
